TPU v7x, 256 devices: a whole 4x4x8 slice. The times are simulated.
256 devices in a mesh: grp: 8 (over z_lo, x), dev: 32 (over z_hi, y, core).
Axes of the slice: x: 4, y: 4, z: 8 (z_hi: 4, z_lo: 2; z = z_hi * 2 + z_lo), core: 2. Of those that a mesh axis runs over, the one named last changes fastest.
Arguments:
- pair_ft: bfloat16 [8192, 2, 4096], P('dev', None, 'grp'), may hold values from -6 to 6
- aux_ft: bfloat16 [4096, 2, 4096], P('dev', None, 'grp'), may hold values from -0.0625 to 0.0625
- coul_weight: float32 [4096], P('grp'), may hold values from 0.2 to 5
- aux_basis: bfloat16 [128, 4096], replicated, may hold values from -0.5 to 0.5
- aux_decay: float32 [4096], replicated, may hold values from 0.05 to 1
- image_dist: float32 [125], replicated, may hold values from 0 to 3
- image_phase: float32 [125], replicated, may hold values from -3.140625 to 3.140625
- item_pair: bfloat16 [4096, 128, 128], P(('grp', 'dev')), may hold values from -4 to 4
- item_image: int32 [4096], P(('grp', 'dev')), may hold values from 0 to 124
- item_sub: int32 [4096], P(('grp', 'dev')), may hold values from 0 to 1
- item_count: int32 [256], P(('grp', 'dev')), may hold values from 0 to 16, as said below
Outputs:
- j3c: bfloat16 [4096, 2, 8192], P('grp', None, 'dev')
Inputs may be any that keep to these rules, and one draw needn't show every extreme that they name: `item_count`: in every index of dev one of the 8 devices holds exactly 16 live slots. The counts of the 8 devices that share an index of dev sum to at most 72, and in every draw some index of dev reaches 72.
All inputs are finite; a program needn't handle non-finite values.
Results may differ from a plain program's by a relative error of at most 0.0047.
Values may be sent and summed in bfloat16 or wider, within the bound.
A program may use at most 64 MiB of HBM per device.

v0:
```python
import math
import jax
import jax.numpy as jnp
from jax import lax
from jax.sharding import PartitionSpec as P


def stacked_pairs(weighted):
    real_part = weighted[:, 0, :].T
    imag_part = weighted[:, 1, :].T
    real_cols = jnp.concatenate([real_part, imag_part], axis=0)
    imag_cols = jnp.concatenate([imag_part, -real_part], axis=0)
    return jnp.concatenate([real_cols, imag_cols], axis=1)


def short_range(
    aux_basis,
    aux_decay,
    image_dist,
    image_phase,
    first_row,
    row_count,
    blocks,
    images,
    sub_ids,
    usable,
    sub_count,
):
    basis_cols = lax.dynamic_slice_in_dim(aux_basis, first_row, row_count, 1)
    decay_rows = lax.dynamic_slice_in_dim(aux_decay, first_row, row_count, 0)
    products = jnp.einsum("kp,ikr->pir", basis_cols, blocks, preferred_element_type=jnp.float32)
    lookup = (images[:, None] == jnp.arange(image_dist.shape[0], dtype=jnp.int32)[None, :]).astype(
        jnp.float32
    )
    distance = jnp.dot(lookup, image_dist, precision=lax.Precision.HIGHEST)
    phase_value = jnp.dot(lookup, image_phase, precision=lax.Precision.HIGHEST)
    damping = jnp.exp(-decay_rows[:, None] * distance[None, :])
    factors = jnp.stack([jnp.cos(phase_value) * usable, jnp.sin(phase_value) * usable], axis=0)
    weights = damping[:, None, :] * factors[None, :, :]
    placing = (sub_ids[:, None] == jnp.arange(sub_count, dtype=jnp.int32)[None, :]).astype(
        jnp.float32
    )
    placed = jnp.einsum(
        "pir,pci,is->pcsr", products, weights, placing, precision=lax.Precision.HIGHEST
    )
    return placed.reshape(row_count, 2, sub_count * products.shape[2])


def body(
    pair_ft,
    aux_ft,
    coul_weight,
    aux_basis,
    aux_decay,
    image_dist,
    image_phase,
    item_pair,
    item_image,
    item_sub,
    item_count,
):
    group_count = lax.axis_size("grp")
    member_count = lax.axis_size("dev")
    capacity = item_image.shape[0]
    local_rows = pair_ft.shape[0]
    sub_rows = item_pair.shape[2]
    sub_count = local_rows // sub_rows
    aux_share = aux_ft.shape[0] * member_count // group_count
    weighted = (pair_ft.astype(jnp.float32) * coul_weight[None, None, :]).astype(jnp.bfloat16)

    def make_term(factors, factor_offset, pair_matrix, blocks, images, sub_ids, usable):

        def term_rows(first_row, row_count):
            block_rows = math.gcd(row_count, 512)

            def one_block(block_index):
                block_start = block_index * block_rows
                local_factors = lax.dynamic_slice_in_dim(
                    factors, block_start - factor_offset, block_rows, 0
                )
                factor_rows = local_factors.reshape(block_rows, -1)
                long_part = jnp.dot(factor_rows, pair_matrix, preferred_element_type=jnp.float32)
                long_part = long_part.reshape(block_rows, 2, local_rows)
                return long_part + short_range(
                    aux_basis,
                    aux_decay,
                    image_dist,
                    image_phase,
                    block_start,
                    block_rows,
                    blocks,
                    images,
                    sub_ids,
                    usable,
                    sub_count,
                )

            pieces = lax.map(one_block, jnp.arange(row_count // block_rows, dtype=jnp.int32))
            return pieces.reshape(row_count, 2, local_rows)

        return term_rows

    gathered = lax.all_gather(aux_ft, "dev", axis=0, tiled=True)
    blocks = item_pair
    images = item_image
    sub_ids = item_sub
    usable = jnp.arange(capacity, dtype=jnp.int32) < item_count[0]
    term_rows = make_term(
        gathered, 0, stacked_pairs(weighted), blocks, images, sub_ids, usable.astype(jnp.float32)
    )
    summed = lax.psum_scatter(
        term_rows(jnp.int32(0), aux_share * lax.axis_size("grp")),
        "grp",
        scatter_dimension=0,
        tiled=True,
    )
    return summed.astype(jnp.bfloat16)


def solution(mesh):
    return jax.shard_map(
        body,
        mesh=mesh,
        in_specs=(
            P("dev", None, "grp"),
            P("dev", None, "grp"),
            P("grp"),
            P(),
            P(),
            P(),
            P(),
            P(("grp", "dev"), None, None),
            P(("grp", "dev")),
            P(("grp", "dev")),
            P(("grp", "dev")),
        ),
        out_specs=P("grp", None, "dev"),
        check_vma=False,
    )
```

profile of v0, /device:TPU:8, one launch (start us, length us, event | category | flops | bytes accessed | tf_op | source)
XLA Modules:
  0.0 434.1 jit_solution(11790446058027590612)
XLA Ops:
  13.8 75.5 %all-gather.2.cloned.1.call-done = bf16[4096,2,512]{2,1,0:T(2,128)(2,1)} async-done(((bf16[128,2,512]{2,1,0:T(2,128)(2,1)}), bf16[4096,2,512]{2,1,0:T(2,128)(2,1)}) %all-gather.2.cloned.1.call-update) | async-done | bytes 8388624 | tf_op jit(solution)/shard_map/all_gather | solution.py:103
  89.3 161.8 %while.14 = (s32[]{:T(128)}, f32[8,512,2,256]{3,2,1,0:T(2,128)}, s32[8]{0:T(128)S(1)}, bf16[4096,2,512]{2,1,0:T(2,128)(2,1)}, bf16[1024,512]{0,1:T(8,128)(2,1)},...) while((s32[]{:T(128)}, f32[8,512,2,256]{3,2,1,0:T(2,128)}, ...), condition=%wide.region_1.2_spmd, body=%wide.region_0.1_spmd.sunk | while | flops 855958080 | bytes 25042132 | solution.py:98
  93.6 8.0 %fusion.38 = f32[512,2,2,128]{3,1,2,0:T(2,128)S(1)} fusion(f32[512,16,128,1]{2,0,1,3:T(8,128)S(1)} %convolution_bitcast_fusion.4, f32[16,512,2]{0,2,1:T(2,128)S(1)} %multiply_bitcast_fusion.2, f32[16,2]{0,1:T(2,128)S(1)} %compare_convert_fusion.2), kind=kOutput, calls=%fused_computation.3.clone.1 | convolution fusion | flops 50364416 | bytes 5308544 | tf_op jit(solution)/shard_map/while/body/eval_jaxpr/pir,pci,is->pcsr/dot_general | solution.py:43
  103.0 2.0 constant_dynamic-slice_fusion.2
  105.8 2.0 fusion.39
  113.9 8.0 %fusion.38 = f32[512,2,2,128]{3,1,2,0:T(2,128)S(1)} fusion(f32[512,16,128,1]{2,0,1,3:T(8,128)S(1)} %convolution_bitcast_fusion.4, f32[16,512,2]{0,2,1:T(2,128)S(1)} %multiply_bitcast_fusion.2, f32[16,2]{0,1:T(2,128)S(1)} %compare_convert_fusion.2), kind=kOutput, calls=%fused_computation.3.clone.1 | convolution fusion | flops 50364416 | bytes 5308544 | tf_op jit(solution)/shard_map/while/body/eval_jaxpr/pir,pci,is->pcsr/dot_general | solution.py:43
  123.3 2.0 constant_dynamic-slice_fusion.2
  126.0 2.0 fusion.39
  134.1 8.0 %fusion.38 = f32[512,2,2,128]{3,1,2,0:T(2,128)S(1)} fusion(f32[512,16,128,1]{2,0,1,3:T(8,128)S(1)} %convolution_bitcast_fusion.4, f32[16,512,2]{0,2,1:T(2,128)S(1)} %multiply_bitcast_fusion.2, f32[16,2]{0,1:T(2,128)S(1)} %compare_convert_fusion.2), kind=kOutput, calls=%fused_computation.3.clone.1 | convolution fusion | flops 50364416 | bytes 5308544 | tf_op jit(solution)/shard_map/while/body/eval_jaxpr/pir,pci,is->pcsr/dot_general | solution.py:43
  143.5 2.0 constant_dynamic-slice_fusion.2
  146.2 2.0 fusion.39
  154.3 8.0 %fusion.38 = f32[512,2,2,128]{3,1,2,0:T(2,128)S(1)} fusion(f32[512,16,128,1]{2,0,1,3:T(8,128)S(1)} %convolution_bitcast_fusion.4, f32[16,512,2]{0,2,1:T(2,128)S(1)} %multiply_bitcast_fusion.2, f32[16,2]{0,1:T(2,128)S(1)} %compare_convert_fusion.2), kind=kOutput, calls=%fused_computation.3.clone.1 | convolution fusion | flops 50364416 | bytes 5308544 | tf_op jit(solution)/shard_map/while/body/eval_jaxpr/pir,pci,is->pcsr/dot_general | solution.py:43
  163.7 2.0 constant_dynamic-slice_fusion.2
  166.4 2.0 fusion.39
  174.5 8.0 %fusion.38 = f32[512,2,2,128]{3,1,2,0:T(2,128)S(1)} fusion(f32[512,16,128,1]{2,0,1,3:T(8,128)S(1)} %convolution_bitcast_fusion.4, f32[16,512,2]{0,2,1:T(2,128)S(1)} %multiply_bitcast_fusion.2, f32[16,2]{0,1:T(2,128)S(1)} %compare_convert_fusion.2), kind=kOutput, calls=%fused_computation.3.clone.1 | convolution fusion | flops 50364416 | bytes 5308544 | tf_op jit(solution)/shard_map/while/body/eval_jaxpr/pir,pci,is->pcsr/dot_general | solution.py:43
  186.7 2.0 fusion.39
  194.8 8.0 %fusion.38 = f32[512,2,2,128]{3,1,2,0:T(2,128)S(1)} fusion(f32[512,16,128,1]{2,0,1,3:T(8,128)S(1)} %convolution_bitcast_fusion.4, f32[16,512,2]{0,2,1:T(2,128)S(1)} %multiply_bitcast_fusion.2, f32[16,2]{0,1:T(2,128)S(1)} %compare_convert_fusion.2), kind=kOutput, calls=%fused_computation.3.clone.1 | convolution fusion | flops 50364416 | bytes 5308544 | tf_op jit(solution)/shard_map/while/body/eval_jaxpr/pir,pci,is->pcsr/dot_general | solution.py:43
  206.9 2.0 fusion.39
  215.0 8.0 %fusion.38 = f32[512,2,2,128]{3,1,2,0:T(2,128)S(1)} fusion(f32[512,16,128,1]{2,0,1,3:T(8,128)S(1)} %convolution_bitcast_fusion.4, f32[16,512,2]{0,2,1:T(2,128)S(1)} %multiply_bitcast_fusion.2, f32[16,2]{0,1:T(2,128)S(1)} %compare_convert_fusion.2), kind=kOutput, calls=%fused_computation.3.clone.1 | convolution fusion | flops 50364416 | bytes 5308544 | tf_op jit(solution)/shard_map/while/body/eval_jaxpr/pir,pci,is->pcsr/dot_general | solution.py:43
  227.1 2.0 fusion.39
  235.2 8.0 %fusion.38 = f32[512,2,2,128]{3,1,2,0:T(2,128)S(1)} fusion(f32[512,16,128,1]{2,0,1,3:T(8,128)S(1)} %convolution_bitcast_fusion.4, f32[16,512,2]{0,2,1:T(2,128)S(1)} %multiply_bitcast_fusion.2, f32[16,2]{0,1:T(2,128)S(1)} %compare_convert_fusion.2), kind=kOutput, calls=%fused_computation.3.clone.1 | convolution fusion | flops 50364416 | bytes 5308544 | tf_op jit(solution)/shard_map/while/body/eval_jaxpr/pir,pci,is->pcsr/dot_general | solution.py:43
  247.4 2.0 fusion.39
  251.2 173.9 %all-reduce.2 = bf16[4096,2,256]{2,1,0:T(2,128)(2,1)} all-reduce(f32[4096,2,256]{2,1,0:T(2,128)} %bitcast.74), channel_id=2, replica_groups=mesh['grp'=8,'dev'=32] {'grp'}, use_global_device_ids=true, to_apply=%region_2.3.clone | all-reduce | flops 2097152 | bytes 12582912
  425.0 2.2 dynamic-slice_convert_fusion
  (108 shorter events, 74.3 us)
Async XLA Ops:
  6.5 3.2 copy-start
  6.5 82.8 %copy-start.1 = (s32[16]{0:T(128)S(1)}, s32[16]{0:T(128)}, u32[]{:S(2)}) copy-start(s32[16]{0:T(128)} %param.22) | copy-start | bytes 196
  6.5 82.8 %all-gather.2.cloned.1.call-start = ((), (), s32[]{:S(2)}) async-start(), calls=%async_computation | async-start | bytes 8650752 | tf_op jit(solution)/shard_map/all_gather | solution.py:103
Sparse Core Ops, SparseCore 0:
  9.9 79.3 all-gather.1
where the time goes:
time: 435 us; the launch traced here: 434 us
  blocking collectives  174 us (40%)
  matrix products  96.5 us (22%)
  waiting for transfers between devices  76.2 us (18%)
  local copies, waits for them, and re-layouts  56.5 us (13%)
  between operations  14.7 us (3%)
  other arithmetic  10.5 us (2%)
  loops' own time  5.75 us (1%)
    unnamed x1, blocking collectives  174 us
    all_gather x1, waiting for transfers between devices, body(): gathered = lax.all_gather(aux_ft, 'dev', axis=0, tiled=True)  75.5 us
    dot_general x8, matrix products, short_range(): jnp.einsum('pir,pci,is->pcsr', products, weights, placing, precision=lax....  64.2 us
    dot_general x8, matrix products, one_block(): jnp.dot(factor_rows, pair_matrix, preferred_element_type=jnp.float32)  15.8 us
    dynamic_slice x8, local copies, waits for them, and re-layouts, one_block(): lax.dynamic_slice_in_dim(factors, block_start - factor_offset, block_rows...  15.6 us
    dot_general x8, matrix products, short_range(): jnp.einsum('kp,ikr->pir', basis_cols, blocks, preferred_element_type=jnp....  14.8 us
    dynamic_update_slice x8, local copies, waits for them, and re-layouts, term_rows(): lax.map(one_block, jnp.arange(row_count // block_rows, dtype=jnp.int32))  14.5 us
  transfers between devices with their start and end apart: 1, of which 1 were waited for; matrix products, arithmetic and copies ran while one was open for 1% of the time, Pallas kernels for 0%

commit v1 on v0

--- a/solution.py
+++ b/solution.py
@@ -100,7 +100,9 @@
 
         return term_rows
 
-    gathered = lax.all_gather(aux_ft, "dev", axis=0, tiled=True)
+    gathered = jnp.concatenate(
+        lax.all_to_all(jnp.stack([aux_ft] * lax.axis_size("dev")), "dev", 0, 0), axis=0
+    )
     blocks = item_pair
     images = item_image
     sub_ids = item_sub

time: 435 us -> 543 us (1.25)
  waiting for transfers between devices: 76.2 us -> 182 us
  between operations: 14.7 us -> 1.47 us
  starting transfers between devices: 0.01 us -> 11.9 us
  local copies, waits for them, and re-layouts: 56.5 us -> 65.4 us
    all_to_all x0 -> x1, waiting for transfers between devices: none -> 182 us  [body(): lax.all_to_all(jnp.stack([aux_ft] * lax.axis_size('dev')), 'dev', 0, 0)]
    all_gather x1 -> x0, waiting for transfers between devices: 75.5 us -> none  [body(): gathered = lax.all_gather(aux_ft, 'dev', axis=0, tiled=True)]
    all_to_all x0 -> x1, starting transfers between devices: none -> 11.9 us  [body(): lax.all_to_all(jnp.stack([aux_ft] * lax.axis_size('dev')), 'dev', 0, 0)]
    another operation x0 -> x1, local copies, waits for them, and re-layouts: none -> 9.52 us  [body(): jnp.stack([aux_ft] * lax.axis_size('dev'))]
  transfers between devices with their start and end apart: 1 -> 1, of which waited for: 1 -> 1; matrix products, arithmetic and copies ran while one was open for 1% -> 0% of each run, Pallas kernels for 0% -> 0%
where the time goes in v1:
time: 543 us; the launch traced here: 542 us
  waiting for transfers between devices  182 us (34%)
  blocking collectives  171 us (31%)
  matrix products  95.2 us (18%)
  local copies, waits for them, and re-layouts  65.4 us (12%)
  starting transfers between devices  11.9 us (2%)
  other arithmetic  9.57 us (2%)
  loops' own time  5.67 us (1%)
    all_to_all x1, waiting for transfers between devices, body(): lax.all_to_all(jnp.stack([aux_ft] * lax.axis_size('dev')), 'dev', 0, 0)  182 us
    unnamed x1, blocking collectives  171 us
    dot_general x8, matrix products, short_range(): jnp.einsum('pir,pci,is->pcsr', products, weights, placing, precision=lax....  64.2 us
    dot_general x8, matrix products, one_block(): jnp.dot(factor_rows, pair_matrix, preferred_element_type=jnp.float32)  15.8 us
    dynamic_slice x8, local copies, waits for them, and re-layouts, one_block(): lax.dynamic_slice_in_dim(factors, block_start - factor_offset, block_rows...  15.6 us
    dot_general x8, matrix products, short_range(): jnp.einsum('kp,ikr->pir', basis_cols, blocks, preferred_element_type=jnp....  14.8 us
    dynamic_update_slice x8, local copies, waits for them, and re-layouts, term_rows(): lax.map(one_block, jnp.arange(row_count // block_rows, dtype=jnp.int32))  14.5 us
    all_to_all x1, starting transfers between devices, body(): lax.all_to_all(jnp.stack([aux_ft] * lax.axis_size('dev')), 'dev', 0, 0)  11.9 us
  transfers between devices with their start and end apart: 1, of which 1 were waited for; matrix products, arithmetic and copies ran while one was open for 0% of the time, Pallas kernels for 0%

profile of v1, /device:TPU:8, one launch (start us, length us, event | category | flops | bytes accessed | tf_op | source)
XLA Modules:
  0.0 542.0 jit_solution(17456101533653970043)
XLA Ops:
  0.0 9.5 %stack.10 = bf16[32,128,2,512]{3,2,1,0:T(2,128)(2,1)} broadcast(bf16[128,2,512]{2,1,0:T(2,128)(2,1)} %param.14), dimensions={1,2,3} | broadcast | bytes 8650752 | tf_op jit(solution)/shard_map/stack | solution.py:104
  9.6 11.9 %all-to-all-start = ((bf16[32,128,2,512]{3,2,1,0:T(2,128)(2,1)}), bf16[32,128,2,512]{3,2,1,0:T(2,128)(2,1)}, u32[]{:S(2)}, u32[]{:S(2)}) async-start(bf16[32,128,2,512]{3,2,1,0:T(2,128)(2,1)} %stack.10), calls=%async_computation | async-start | bytes 16777216 | tf_op jit(solution)/shard_map/all_to_all | solution.py:104
  25.3 182.0 %all-to-all-done = bf16[32,128,2,512]{3,2,1,0:T(2,128)(2,1)} async-done(((bf16[32,128,2,512]{3,2,1,0:T(2,128)(2,1)}), bf16[32,128,2,512]{3,2,1,0:T(2,128)(2,1)}, u32[]{:S(2)}, u32[]{:S(2)}) %all-to-all-start) | async-done | bytes 8388640 | tf_op jit(solution)/shard_map/all_to_all | solution.py:104
  207.3 161.7 %while.14 = (s32[]{:T(128)}, f32[8,512,2,256]{3,2,1,0:T(2,128)}, s32[8]{0:T(128)S(1)}, bf16[4096,2,512]{2,1,0:T(2,128)(2,1)}, bf16[1024,512]{0,1:T(8,128)(2,1)},...) while((s32[]{:T(128)}, f32[8,512,2,256]{3,2,1,0:T(2,128)}, ...), condition=%wide.region_1.2_spmd, body=%wide.region_0.1_spmd.sunk | while | flops 855958080 | bytes 25042132 | solution.py:98
  211.6 8.0 %fusion.38 = f32[512,2,2,128]{3,1,2,0:T(2,128)S(1)} fusion(f32[512,16,128,1]{2,0,1,3:T(8,128)S(1)} %convolution_bitcast_fusion.4, f32[16,512,2]{0,2,1:T(2,128)S(1)} %multiply_bitcast_fusion.2, f32[16,2]{0,1:T(2,128)S(1)} %compare_convert_fusion.2), kind=kOutput, calls=%fused_computation.3.clone.1 | convolution fusion | flops 50364416 | bytes 5308544 | tf_op jit(solution)/shard_map/while/body/eval_jaxpr/pir,pci,is->pcsr/dot_general | solution.py:43
  221.0 2.0 constant_dynamic-slice_fusion.2
  223.8 2.0 fusion.39
  231.9 8.0 %fusion.38 = f32[512,2,2,128]{3,1,2,0:T(2,128)S(1)} fusion(f32[512,16,128,1]{2,0,1,3:T(8,128)S(1)} %convolution_bitcast_fusion.4, f32[16,512,2]{0,2,1:T(2,128)S(1)} %multiply_bitcast_fusion.2, f32[16,2]{0,1:T(2,128)S(1)} %compare_convert_fusion.2), kind=kOutput, calls=%fused_computation.3.clone.1 | convolution fusion | flops 50364416 | bytes 5308544 | tf_op jit(solution)/shard_map/while/body/eval_jaxpr/pir,pci,is->pcsr/dot_general | solution.py:43
  241.3 2.0 constant_dynamic-slice_fusion.2
  244.0 2.0 fusion.39
  252.0 8.0 %fusion.38 = f32[512,2,2,128]{3,1,2,0:T(2,128)S(1)} fusion(f32[512,16,128,1]{2,0,1,3:T(8,128)S(1)} %convolution_bitcast_fusion.4, f32[16,512,2]{0,2,1:T(2,128)S(1)} %multiply_bitcast_fusion.2, f32[16,2]{0,1:T(2,128)S(1)} %compare_convert_fusion.2), kind=kOutput, calls=%fused_computation.3.clone.1 | convolution fusion | flops 50364416 | bytes 5308544 | tf_op jit(solution)/shard_map/while/body/eval_jaxpr/pir,pci,is->pcsr/dot_general | solution.py:43
  264.2 2.0 fusion.39
  272.2 8.0 %fusion.38 = f32[512,2,2,128]{3,1,2,0:T(2,128)S(1)} fusion(f32[512,16,128,1]{2,0,1,3:T(8,128)S(1)} %convolution_bitcast_fusion.4, f32[16,512,2]{0,2,1:T(2,128)S(1)} %multiply_bitcast_fusion.2, f32[16,2]{0,1:T(2,128)S(1)} %compare_convert_fusion.2), kind=kOutput, calls=%fused_computation.3.clone.1 | convolution fusion | flops 50364416 | bytes 5308544 | tf_op jit(solution)/shard_map/while/body/eval_jaxpr/pir,pci,is->pcsr/dot_general | solution.py:43
  284.4 2.0 fusion.39
  292.4 8.0 %fusion.38 = f32[512,2,2,128]{3,1,2,0:T(2,128)S(1)} fusion(f32[512,16,128,1]{2,0,1,3:T(8,128)S(1)} %convolution_bitcast_fusion.4, f32[16,512,2]{0,2,1:T(2,128)S(1)} %multiply_bitcast_fusion.2, f32[16,2]{0,1:T(2,128)S(1)} %compare_convert_fusion.2), kind=kOutput, calls=%fused_computation.3.clone.1 | convolution fusion | flops 50364416 | bytes 5308544 | tf_op jit(solution)/shard_map/while/body/eval_jaxpr/pir,pci,is->pcsr/dot_general | solution.py:43
  304.6 2.0 fusion.39
  312.7 8.0 %fusion.38 = f32[512,2,2,128]{3,1,2,0:T(2,128)S(1)} fusion(f32[512,16,128,1]{2,0,1,3:T(8,128)S(1)} %convolution_bitcast_fusion.4, f32[16,512,2]{0,2,1:T(2,128)S(1)} %multiply_bitcast_fusion.2, f32[16,2]{0,1:T(2,128)S(1)} %compare_convert_fusion.2), kind=kOutput, calls=%fused_computation.3.clone.1 | convolution fusion | flops 50364416 | bytes 5308544 | tf_op jit(solution)/shard_map/while/body/eval_jaxpr/pir,pci,is->pcsr/dot_general | solution.py:43
  324.9 2.0 fusion.39
  332.9 8.0 %fusion.38 = f32[512,2,2,128]{3,1,2,0:T(2,128)S(1)} fusion(f32[512,16,128,1]{2,0,1,3:T(8,128)S(1)} %convolution_bitcast_fusion.4, f32[16,512,2]{0,2,1:T(2,128)S(1)} %multiply_bitcast_fusion.2, f32[16,2]{0,1:T(2,128)S(1)} %compare_convert_fusion.2), kind=kOutput, calls=%fused_computation.3.clone.1 | convolution fusion | flops 50364416 | bytes 5308544 | tf_op jit(solution)/shard_map/while/body/eval_jaxpr/pir,pci,is->pcsr/dot_general | solution.py:43
  345.0 2.0 fusion.39
  353.1 8.0 %fusion.38 = f32[512,2,2,128]{3,1,2,0:T(2,128)S(1)} fusion(f32[512,16,128,1]{2,0,1,3:T(8,128)S(1)} %convolution_bitcast_fusion.4, f32[16,512,2]{0,2,1:T(2,128)S(1)} %multiply_bitcast_fusion.2, f32[16,2]{0,1:T(2,128)S(1)} %compare_convert_fusion.2), kind=kOutput, calls=%fused_computation.3.clone.1 | convolution fusion | flops 50364416 | bytes 5308544 | tf_op jit(solution)/shard_map/while/body/eval_jaxpr/pir,pci,is->pcsr/dot_general | solution.py:43
  365.2 2.0 fusion.39
  369.0 170.8 %all-reduce.2 = bf16[4096,2,256]{2,1,0:T(2,128)(2,1)} all-reduce(f32[4096,2,256]{2,1,0:T(2,128)} %bitcast.75), channel_id=2, replica_groups=mesh['grp'=8,'dev'=32] {'grp'}, use_global_device_ids=true, to_apply=%region_2.3.clone | all-reduce | flops 2097152 | bytes 12582912
  539.8 2.2 dynamic-slice_convert_fusion
  (118 shorter events, 74.6 us)
Async XLA Ops:
  0.0 23.5 %copy-start = (f32[125]{0:T(128)S(1)}, f32[125]{0:T(128)}, u32[]{:S(2)}) copy-start(f32[125]{0:T(128)} %param.19) | copy-start | bytes 1504
  9.5 12.6 %copy-start.6 = (u32[256]{0:T(256)S(1)}, u32[256]{0:T(256)}, u32[]{:S(2)}) copy-start(u32[256]{0:T(256)} %constant.47) | copy-start | bytes 3076
  9.5 14.0 %copy-start.3 = (s32[16]{0:T(128)S(1)}, s32[16]{0:T(128)}, u32[]{:S(2)}) copy-start(s32[16]{0:T(128)} %param.21) | copy-start | bytes 196
  9.5 14.3 %copy-start.4 = (f32[125]{0:T(128)S(1)}, f32[125]{0:T(128)}, u32[]{:S(2)}) copy-start(f32[125]{0:T(128)} %param.18) | copy-start | bytes 1504
  9.5 14.4 %copy-start.1 = (bf16[256,2,512]{2,1,0:T(2,128)(2,1)S(1)}, bf16[256,2,512]{2,1,0:T(2,128)(2,1)}, u32[]{:S(2)}) copy-start(bf16[256,2,512]{2,1,0:T(2,128)(2,1)} %param.13) | copy-start | bytes 1572868
  9.6 14.4 %copy-start.2 = (f32[512]{0:T(512)S(1)}, f32[512]{0:T(512)}, u32[]{:S(2)}) copy-start(f32[512]{0:T(512)} %param.15) | copy-start | bytes 6148
  9.6 197.8 %all-to-all-start = ((bf16[32,128,2,512]{3,2,1,0:T(2,128)(2,1)}), bf16[32,128,2,512]{3,2,1,0:T(2,128)(2,1)}, u32[]{:S(2)}, u32[]{:S(2)}) async-start(bf16[32,128,2,512]{3,2,1,0:T(2,128)(2,1)} %stack.10), calls=%async_computation | async-start | bytes 16777216 | tf_op jit(solution)/shard_map/all_to_all | solution.py:104
  21.5 185.9 %copy-start.5 = (s32[16]{0:T(128)S(1)}, s32[16]{0:T(128)}, u32[]{:S(2)}) copy-start(s32[16]{0:T(128)} %param.22) | copy-start | bytes 196
